TPU v7x, 32 devices: a whole 2x2x4 slice. The times are simulated.
32 devices in a mesh: replica: 8 (over z, core), group: 4 (over y, x).
Axes of the slice: x: 2, y: 2, z: 4, core: 2. Of those that a mesh axis runs over, the one named last changes fastest.
Arguments:
- tokens: bfloat16 [4, 8192, 768], P('group', 'replica'), may hold values from -6 to 6
- cotangent: bfloat16 [4, 8192, 768], P('group', 'replica'), may hold values from -6 to 6
- lengths: int32 [4, 16], P('group'), may hold values from 256 to 768, as said below
- dealing: int32 [4, 16], P('group'), may hold values from 0 to 15, as said below
- offsets: int32 [4, 8, 2], P('group'), may hold values from 0 to 768, as said below
- attn_gain: float32 [768], P('group'), may hold values from 0.1 to 1.9
- qkv_weight: float32 [768, 2304], P('group'), may hold values from -0.21875 to 0.21875
- out_weight: float32 [768, 768], P('group'), may hold values from -0.875 to 0.875
- mlp_gain: float32 [768], P('group'), may hold values from 0.1 to 1.9
- in_weight: float32 [768, 2304], P('group'), may hold values from -0.21875 to 0.21875
- down_weight: float32 [1152, 768], P('group'), may hold values from -0.1875 to 0.1875
Outputs:
- output: bfloat16 [4, 8192, 768], P('group', 'replica')
- input_grad: bfloat16 [4, 8192, 768], P('group', 'replica')
- attn_gain_grad: float32 [768], P('group')
- qkv_grad: float32 [768, 2304], P('group')
- out_grad: float32 [768, 768], P('group')
- mlp_gain_grad: float32 [768], P('group')
- in_grad: float32 [768, 2304], P('group')
- down_grad: float32 [1152, 768], P('group')
Inputs may be any that keep to these rules, and one draw needn't show every extreme that they name: `lengths`: the 16 sequences of a column lie end to end over its 8192 tokens; the two sequences dealt to one replica index hold 1024 tokens together. `dealing`: for each column a permutation of its sequences: entry k is the given-order number of the sequence that is k-th in dealt order; replica index r takes dealt sequences 2 * r to 2 * r + 1. `offsets`: exclusive running sums of the lengths of each replica index's dealt sequences, in dealt order.
All inputs are finite; a program needn't handle non-finite values.
Results may differ from a plain program's by a relative error of at most 0.02.
Values may be sent and summed in bfloat16 or wider, within the bound.
No kernel may reach another device: no remote copies, remote signals or barrier semaphores. Data moves between devices by JAX's collectives and lax.ppermute only.
A program may use at most 256 MiB of HBM per device.

v0:
```python
import math
import jax
import jax.numpy as jnp
from jax import lax
from jax.sharding import PartitionSpec as P

HEADS = 12
HEAD_DIM = 64
epsilon = 1e-05
big_negative = -1e30
rope_base = 160000.0


def column_starts(lengths):
    return jnp.cumsum(lengths) - lengths


def dealt_map(lengths, dealing, offsets, replica_index, tok_rows):
    seq_count = lengths.shape[0]
    per_device = offsets.shape[1]
    starts = column_starts(lengths)
    slot_ids = jnp.arange(tok_rows, dtype=jnp.int32)
    own_starts = lax.dynamic_index_in_dim(offsets, replica_index, 0, keepdims=False)
    segment = jnp.sum((slot_ids[:, None] >= own_starts[None, 1:]).astype(jnp.int32), axis=1)
    choose = segment[:, None] == jnp.arange(per_device, dtype=jnp.int32)[None, :]
    begin_at = jnp.sum(jnp.where(choose, own_starts[None, :], 0), axis=1)
    positions = slot_ids - begin_at
    dealt = replica_index * per_device + segment
    seq_range = jnp.arange(seq_count, dtype=jnp.int32)
    dealt_hits = dealt[:, None] == seq_range[None, :]
    given = jnp.sum(jnp.where(dealt_hits, dealing[None, :], 0), axis=1)
    found_seq = given[:, None] == seq_range[None, :]
    first_at = jnp.sum(jnp.where(found_seq, starts[None, :], 0), axis=1)
    source = jnp.clip(first_at + positions, 0, tok_rows * offsets.shape[0] - 1)
    return (source, segment, positions)


def given_map(lengths, dealing, offsets, column_pos, tok_rows):
    seq_count = lengths.shape[0]
    per_device = offsets.shape[1]
    starts = column_starts(lengths)
    seq_range = jnp.arange(seq_count, dtype=jnp.int32)
    seq_id = jnp.sum((column_pos[:, None] >= starts[None, 1:]).astype(jnp.int32), axis=1)
    found_seq = seq_id[:, None] == seq_range[None, :]
    first_at = jnp.sum(jnp.where(found_seq, starts[None, :], 0), axis=1)
    positions = column_pos - first_at
    matches = dealing[None, :] == seq_id[:, None]
    dealt = jnp.sum(jnp.where(matches, seq_range[None, :], 0), axis=1)
    flat_starts = offsets.reshape(-1)
    dealt_hits = dealt[:, None] == seq_range[None, :]
    begin_at = jnp.sum(jnp.where(dealt_hits, flat_starts[None, :], 0), axis=1)
    target = dealt // per_device * tok_rows + begin_at + positions
    return jnp.clip(target, 0, tok_rows * offsets.shape[0] - 1)


def rotary(values, positions, head_count, head_dim):
    tok_rows = values.shape[0]
    half_dim = head_dim // 2
    frequency = jnp.exp(
        -(jnp.arange(half_dim, dtype=jnp.float32) * (2.0 / head_dim)) * math.log(rope_base)
    )
    angles = positions.astype(jnp.float32)[:, None] * frequency[None, :]
    cosine = jnp.cos(angles)[:, None, :]
    sine_part = jnp.sin(angles)[:, None, :]
    shaped = values.reshape(tok_rows, head_count, head_dim)
    lower_half = shaped[..., :half_dim]
    upper_half = shaped[..., half_dim:]
    turned = jnp.concatenate(
        [
            lower_half * cosine - upper_half * sine_part,
            upper_half * cosine + lower_half * sine_part,
        ],
        axis=-1,
    )
    return turned.reshape(tok_rows, head_count * head_dim)


def layer_norm(values, gain_vec):
    row_mean = jnp.mean(values, axis=-1, keepdims=True)
    centred = values - row_mean
    spread = jnp.mean(centred * centred, axis=-1, keepdims=True)
    return centred * lax.rsqrt(spread + epsilon) * gain_vec


def geglu(lifted):
    hidden_width = lifted.shape[1] // 2
    return jax.nn.gelu(lifted[:, :hidden_width], approximate=False) * lifted[:, hidden_width:]


def pick_rows(index_map, carry, piece):
    piece_rows = piece.shape[1]
    inside = (index_map >= 0) & (index_map < piece_rows)
    taken = jnp.take(piece[0], jnp.clip(index_map, 0, piece_rows - 1), axis=0)
    return jnp.where(inside[:, None], taken, carry)


def soft_block(queries, seg_query, key_heads, segment, score_scale):
    scores = (
        jnp.einsum("qhd,khd->hqk", queries, key_heads, preferred_element_type=jnp.float32)
        * score_scale
    )
    same_seq = seg_query[:, None] == segment[None, :]
    return jnp.where(same_seq[None], scores, big_negative)


def on_device(
    tokens,
    cotangent,
    lengths,
    dealing,
    offsets,
    attn_gain,
    qkv_weight,
    out_weight,
    mlp_gain,
    in_weight,
    down_weight,
):
    tok_rows = tokens.shape[1]
    model_width = tokens.shape[2]
    head_count = HEADS
    head_dim = HEAD_DIM
    score_scale = head_dim ** (-0.5)
    replica_index = lax.axis_index("replica")
    source, segment, positions = dealt_map(
        lengths[0], dealing[0], offsets[0], replica_index, tok_rows
    )
    target = given_map(
        lengths[0],
        dealing[0],
        offsets[0],
        replica_index * tok_rows + jnp.arange(tok_rows, dtype=jnp.int32),
        tok_rows,
    )
    masters = (
        attn_gain.astype(jnp.bfloat16),
        qkv_weight.astype(jnp.bfloat16),
        out_weight.astype(jnp.bfloat16),
        mlp_gain.astype(jnp.bfloat16),
        in_weight.astype(jnp.bfloat16),
        down_weight.astype(jnp.bfloat16),
    )
    weights = (
        lax.all_gather(masters[0], "group", axis=0, tiled=True),
        lax.all_gather(masters[1], "group", axis=0, tiled=True),
        lax.all_gather(masters[2], "group", axis=0, tiled=True),
        lax.all_gather(masters[3], "group", axis=0, tiled=True),
        lax.all_gather(masters[4], "group", axis=0, tiled=True),
        lax.all_gather(masters[5], "group", axis=0, tiled=True),
    )
    blank = jnp.zeros((tok_rows, model_width), jnp.bfloat16)
    dealt_x = pick_rows(source, blank, lax.all_gather(tokens, "replica", axis=1, tiled=True))
    gain_one, w_qkv, w_out, gain_two, w_in, w_down = weights
    gain_first = gain_one.astype(jnp.float32)
    gain_second = gain_two.astype(jnp.float32)
    rows_in = dealt_x.astype(jnp.float32)
    normed = layer_norm(rows_in, gain_first).astype(jnp.bfloat16)
    mixed_proj = jnp.dot(normed, w_qkv, preferred_element_type=jnp.float32)
    queries = (
        rotary(mixed_proj[:, :model_width], positions, head_count, head_dim)
        .astype(jnp.bfloat16)
        .reshape(tok_rows, head_count, head_dim)
    )
    key_heads = (
        rotary(mixed_proj[:, model_width : 2 * model_width], positions, head_count, head_dim)
        .astype(jnp.bfloat16)
        .reshape(tok_rows, head_count, head_dim)
    )
    value_heads = (
        mixed_proj[:, 2 * model_width :]
        .astype(jnp.bfloat16)
        .reshape(tok_rows, head_count, head_dim)
    )
    block_rows = min(512, tok_rows)
    block_count = tok_rows // block_rows
    attended_parts = []
    kept_tops = []
    kept_totals = []
    for number in range(block_count):
        lower_row = number * block_rows
        masked = soft_block(
            queries[lower_row : lower_row + block_rows],
            segment[lower_row : lower_row + block_rows],
            key_heads,
            segment,
            score_scale,
        )
        row_top = jnp.max(masked, axis=-1, keepdims=True)
        exponent = jnp.exp(masked - row_top)
        row_total = jnp.sum(exponent, axis=-1, keepdims=True)
        weights_soft = (exponent / row_total).astype(jnp.bfloat16)
        attended_block = jnp.einsum(
            "hqk,khd->qhd", weights_soft, value_heads, preferred_element_type=jnp.float32
        )
        attended_parts.append(attended_block.astype(jnp.bfloat16))
        kept_tops.append(row_top)
        kept_totals.append(row_total)
    attended = jnp.concatenate(attended_parts, axis=0).reshape(tok_rows, model_width)
    middle = rows_in + jnp.dot(attended, w_out, preferred_element_type=jnp.float32)
    normed_two = layer_norm(middle, gain_second).astype(jnp.bfloat16)
    lifted = jnp.dot(normed_two, w_in, preferred_element_type=jnp.float32)
    hidden = geglu(lifted).astype(jnp.bfloat16)
    output_dealt = (middle + jnp.dot(hidden, w_down, preferred_element_type=jnp.float32)).astype(
        jnp.bfloat16
    )
    output_given = pick_rows(
        target, blank, lax.all_gather(output_dealt[None], "replica", axis=1, tiled=True)
    )
    dealt_dy = pick_rows(source, blank, lax.all_gather(cotangent, "replica", axis=1, tiled=True))
    weights = (
        lax.all_gather(masters[0], "group", axis=0, tiled=True),
        lax.all_gather(masters[1], "group", axis=0, tiled=True),
        lax.all_gather(masters[2], "group", axis=0, tiled=True),
        lax.all_gather(masters[3], "group", axis=0, tiled=True),
        lax.all_gather(masters[4], "group", axis=0, tiled=True),
        lax.all_gather(masters[5], "group", axis=0, tiled=True),
    )
    gain_one, w_qkv, w_out, gain_two, w_in, w_down = weights
    grad_out = dealt_dy.astype(jnp.float32)
    down_partial = jnp.einsum("tf,td->fd", hidden, dealt_dy, preferred_element_type=jnp.float32)
    grad_hidden = jnp.einsum("td,fd->tf", dealt_dy, w_down, preferred_element_type=jnp.float32)
    _, geglu_back = jax.vjp(geglu, lifted)
    grad_lifted = geglu_back(grad_hidden)[0].astype(jnp.bfloat16)
    in_partial = jnp.einsum(
        "td,tf->df", normed_two, grad_lifted, preferred_element_type=jnp.float32
    )
    grad_normed_two = jnp.einsum("tf,df->td", grad_lifted, w_in, preferred_element_type=jnp.float32)
    _, norm_back_two = jax.vjp(layer_norm, middle, gain_second)
    grad_middle_part, gain_two_partial = norm_back_two(grad_normed_two)
    grad_middle = grad_out + grad_middle_part
    grad_branch = grad_middle.astype(jnp.bfloat16)
    out_partial = jnp.einsum("ti,to->io", attended, grad_branch, preferred_element_type=jnp.float32)
    grad_attended = (
        jnp.einsum("to,io->ti", grad_branch, w_out, preferred_element_type=jnp.float32)
        .astype(jnp.bfloat16)
        .reshape(tok_rows, head_count, head_dim)
    )
    grad_keys = jnp.zeros((tok_rows, head_count, head_dim), jnp.float32)
    grad_values = jnp.zeros((tok_rows, head_count, head_dim), jnp.float32)
    grad_query_parts = []
    for number in range(block_count):
        lower_row = number * block_rows
        query_block = queries[lower_row : lower_row + block_rows]
        masked = soft_block(
            query_block,
            segment[lower_row : lower_row + block_rows],
            key_heads,
            segment,
            score_scale,
        )
        weights_full = jnp.exp(masked - kept_tops[number]) / kept_totals[number]
        weights_soft = weights_full.astype(jnp.bfloat16)
        grad_block = grad_attended[lower_row : lower_row + block_rows]
        grad_probs = jnp.einsum(
            "qhd,khd->hqk", grad_block, value_heads, preferred_element_type=jnp.float32
        )
        inner = jnp.sum(weights_full * grad_probs, axis=-1, keepdims=True)
        grad_scores = (weights_full * (grad_probs - inner)).astype(jnp.bfloat16)
        grad_query_parts.append(
            jnp.einsum("hqk,khd->qhd", grad_scores, key_heads, preferred_element_type=jnp.float32)
            * score_scale
        )
        grad_keys = (
            grad_keys
            + jnp.einsum(
                "hqk,qhd->khd", grad_scores, query_block, preferred_element_type=jnp.float32
            )
            * score_scale
        )
        grad_values = grad_values + jnp.einsum(
            "hqk,qhd->khd", weights_soft, grad_block, preferred_element_type=jnp.float32
        )
    grad_queries = jnp.concatenate(grad_query_parts, axis=0).reshape(tok_rows, model_width)

    def turn_rows(values):
        return rotary(values, positions, head_count, head_dim)

    _, rope_back = jax.vjp(turn_rows, mixed_proj[:, :model_width])
    grad_mixed = jnp.concatenate(
        [
            rope_back(grad_queries)[0],
            rope_back(grad_keys.reshape(tok_rows, model_width))[0],
            grad_values.reshape(tok_rows, model_width),
        ],
        axis=1,
    ).astype(jnp.bfloat16)
    qkv_partial = jnp.einsum("td,te->de", normed, grad_mixed, preferred_element_type=jnp.float32)
    grad_normed = jnp.einsum("te,de->td", grad_mixed, w_qkv, preferred_element_type=jnp.float32)
    _, norm_back_one = jax.vjp(layer_norm, rows_in, gain_first)
    grad_rows_part, gain_one_partial = norm_back_one(grad_normed)
    grad_input = (grad_middle + grad_rows_part).astype(jnp.bfloat16)
    grad_given = pick_rows(
        target, blank, lax.all_gather(grad_input[None], "replica", axis=1, tiled=True)
    )
    partial_grads = (
        gain_one_partial,
        qkv_partial,
        out_partial,
        gain_two_partial,
        in_partial,
        down_partial,
    )
    shards = (
        lax.psum_scatter(
            partial_grads[0].astype(jnp.bfloat16), "group", scatter_dimension=0, tiled=True
        ).astype(jnp.float32),
        lax.psum_scatter(
            partial_grads[1].astype(jnp.bfloat16), "group", scatter_dimension=0, tiled=True
        ).astype(jnp.float32),
        lax.psum_scatter(
            partial_grads[2].astype(jnp.bfloat16), "group", scatter_dimension=0, tiled=True
        ).astype(jnp.float32),
        lax.psum_scatter(
            partial_grads[3].astype(jnp.bfloat16), "group", scatter_dimension=0, tiled=True
        ).astype(jnp.float32),
        lax.psum_scatter(
            partial_grads[4].astype(jnp.bfloat16), "group", scatter_dimension=0, tiled=True
        ).astype(jnp.float32),
        lax.psum_scatter(
            partial_grads[5].astype(jnp.bfloat16), "group", scatter_dimension=0, tiled=True
        ).astype(jnp.float32),
    )
    summed = (
        lax.psum(shards[0].astype(jnp.bfloat16), "replica").astype(jnp.float32),
        lax.psum(shards[1].astype(jnp.bfloat16), "replica").astype(jnp.float32),
        lax.psum(shards[2].astype(jnp.bfloat16), "replica").astype(jnp.float32),
        lax.psum(shards[3].astype(jnp.bfloat16), "replica").astype(jnp.float32),
        lax.psum(shards[4].astype(jnp.bfloat16), "replica").astype(jnp.float32),
        lax.psum(shards[5].astype(jnp.bfloat16), "replica").astype(jnp.float32),
    )
    return (
        output_given[None],
        grad_given[None],
        summed[0],
        summed[1],
        summed[2],
        summed[3],
        summed[4],
        summed[5],
    )


def solution(mesh):
    return jax.shard_map(
        on_device,
        mesh=mesh,
        in_specs=(
            P("group", "replica", None),
            P("group", "replica", None),
            P("group", None),
            P("group", None),
            P("group", None, None),
            P("group"),
            P("group", None),
            P("group", None),
            P("group"),
            P("group", None),
            P("group", None),
        ),
        out_specs=(
            P("group", "replica", None),
            P("group", "replica", None),
            P("group"),
            P("group", None),
            P("group", None),
            P("group"),
            P("group", None),
            P("group", None),
        ),
        check_vma=False,
    )
```

profile of v0, /device:TPU:0, one launch (start us, length us, event | category | flops | bytes accessed | tf_op | source)
XLA Modules:
  0.0 1018.6 jit_solution(18329896838933659207)
XLA Ops:
  8.0 2.6 convert_element_type.175
  21.5 11.4 %all-reduce.13 = (bf16[768]{0:T(1024)(128)(2,1)S(1)}, bf16[768]{0:T(1024)(128)(2,1)S(1)}) all-reduce(bf16[768]{0:T(1024)(128)(2,1)S(1)} %dynamic-update-slice, bf16[768]{0:T(1024)(128)(2,1)S(1)} %dynamic-update-slice.1), channel_id=1, replica_groups=mesh['replica'=8,'group'=4] {'group'}, use_global_device_ids=true, to_apply=%add.6 | all-reduce | flops 1536 | bytes 6144
  35.0 94.1 %all-gather.11.cloned.1.call-done = bf16[1,8192,768]{2,1,0:T(8,128)(2,1)} async-done(((bf16[1,1024,768]{2,1,0:T(8,128)(2,1)}), bf16[1,8192,768]{2,1,0:T(8,128)(2,1)}) %all-gather.11.cloned.1.call-update) | async-done | bytes 12582928 | tf_op jit(solution)/shard_map/all_gather | solution.py:152
  129.1 10.7 %gather_fusion = bf16[1024,768]{1,0:T(8,128)(2,1)S(1)} fusion(bf16[8192,768]{1,0:T(8,128)(2,1)} %bitcast.69, s32[1024]{0:T(1024)S(1)} %get-tuple-element.93), kind=kCustom, calls=%fused_computation.clone | custom fusion | bytes 3149824 | tf_op jit(solution)/shard_map/jit(_take)/gather | solution.py:93
  141.7 35.2 %all-gather.13.cloned.1.call-done = bf16[768,2304]{1,0:T(8,128)(2,1)} async-done(((bf16[192,2304]{1,0:T(8,128)(2,1)}), bf16[768,2304]{1,0:T(8,128)(2,1)}) %all-gather.13.cloned.1.call-update) | async-done | bytes 3538960 | tf_op jit(solution)/shard_map/all_gather | solution.py:145
  176.9 6.2 fusion.60
  183.3 3.2 fusion.104
  186.5 4.0 copy.71
  192.1 3.5 copy.70
  195.6 3.9 subtract_convert_fusion
  199.6 10.4 %fusion.62 = f32[12,512,1024]{2,1,0:T(8,128)} fusion(bf16[1024,12,32]{0,2,1:T(8,128)(2,1)S(1)} %get-tuple-element.82, bf16[1024,12,32]{0,2,1:T(8,128)(2,1)S(1)} %get-tuple-element.83, bf16[1024,12,32]{0,2,1:T(8,128)(2,1)S(1)} %get-tuple-element.75, bf16[1024,12,32]{0,2,1:T(8,128)(2,1)S(1)} %get-tuple-element.74), kind=kOutput, calls=%fused_computation.126 | convolution fusion | flops 810024960 | bytes 28311552 | tf_op jit(solution)/shard_map/qhd,khd->hqk/dot_general | solution.py:99
  210.0 14.6 %fusion.109 = (f32[12,512]{1,0:T(8,128)S(1)}, f32[12,512,1024]{2,1,0:T(8,128)}) fusion(pred[512,1024]{1,0:T(8,128)(4,1)} %get-tuple-element.88, bf16[1024,12,32]{0,2,1:T(8,128)(2,1)} %copy-done.17, bf16[1024,12,32]{0,2,1:T(8,128)(2,1)} %copy-done.15, bf16[1024,12,32]{0,2,1:T(8,128)(2,1)S(1)} %get-tuple-element.83, ...), kind=kOutput, calls=%fused_computation.205 | convolution fusion | flops 835191808 | bytes 28860416 | tf_op jit(solution)/shard_map/sub | solution.py:189
  224.6 33.6 %fusion.108 = (f32[12,512]{1,0:T(8,128)S(1)}, f32[12,512,1024]{2,1,0:T(8,128)}) fusion(f32[12,512,1024]{2,1,0:T(8,128)} %fusion.62, pred[512,1024]{1,0:T(8,128)(4,1)} %get-tuple-element.89), kind=kOutput, calls=%fused_computation.204 | output fusion | flops 37749760 | bytes 50880512 | tf_op jit(solution)/shard_map/sub | solution.py:189
  258.2 11.4 %fusion.52 = bf16[512,12,64]{0,2,1:T(8,128)(2,1)} fusion(bf16[1024,12,64]{0,2,1:T(8,128)(2,1)S(1)} %bitcast.72, f32[12,512,1024]{2,1,0:T(8,128)} %get-tuple-element.101, f32[12,512]{1,0:T(8,128)S(1)} %get-tuple-element.100), kind=kOutput, calls=%fused_computation.115 | convolution fusion | flops 818282496 | bytes 27549696 | tf_op jit(solution)/shard_map/hqk,khd->qhd/dot_general | solution.py:192
  269.6 11.6 %fusion.49 = bf16[512,12,64]{0,2,1:T(8,128)(2,1)} fusion(bf16[1024,12,64]{0,2,1:T(8,128)(2,1)S(1)} %bitcast.73, f32[12,512,1024]{2,1,0:T(8,128)} %get-tuple-element.99, f32[12,512]{1,0:T(8,128)S(1)} %get-tuple-element.98), kind=kOutput, calls=%fused_computation.114 | convolution fusion | flops 818282496 | bytes 27549696 | tf_op jit(solution)/shard_map/hqk,khd->qhd/dot_general | solution.py:192
  281.2 14.1 %all-gather.21.cloned.1.call-done = bf16[1,8192,768]{2,1,0:T(8,128)(2,1)} async-done(((bf16[1,1024,768]{2,1,0:T(8,128)(2,1)}), bf16[1,8192,768]{2,1,0:T(8,128)(2,1)}) %all-gather.21.cloned.1.call-update) | async-done | bytes 12582928 | tf_op jit(solution)/shard_map/all_gather | solution.py:209
  295.3 11.8 %gather_fusion.2 = bf16[1024,768]{1,0:T(8,128)(2,1)} fusion(bf16[8192,768]{1,0:T(8,128)(2,1)} %bitcast.68, s32[1024]{0:T(1024)S(1)} %get-tuple-element.93), kind=kCustom, calls=%fused_computation.2.clone | custom fusion | bytes 3149824 | tf_op jit(solution)/shard_map/jit(_take)/gather | solution.py:93
  307.0 1.7 copy.75
  308.8 3.3 pad_maximum_fusion.5
  312.0 10.8 %all-gather.15.cloned.1.call-done = bf16[768,768]{1,0:T(8,128)(2,1)} async-done(((bf16[192,768]{1,0:T(8,128)(2,1)}), bf16[768,768]{1,0:T(8,128)(2,1)}) %all-gather.15.cloned.1.call-update) | async-done | bytes 1179664 | tf_op jit(solution)/shard_map/all_gather | solution.py:146
  322.8 3.4 fusion.114
  328.2 44.0 %all-gather.17.cloned.1.call-done = bf16[768,2304]{1,0:T(8,128)(2,1)} async-done(((bf16[192,2304]{1,0:T(8,128)(2,1)}), bf16[768,2304]{1,0:T(8,128)(2,1)}) %all-gather.17.cloned.1.call-update) | async-done | bytes 3538960 | tf_op jit(solution)/shard_map/all_gather | solution.py:148
  372.2 10.6 %fusion.93 = f32[1024,2304]{1,0:T(8,128)} fusion(bf16[768,2304]{1,0:T(8,128)(2,1)} %all-gather.17.cloned.1.call-done, f32[1024,768]{0,1:T(8,128)} %copy-done.12, f32[768]{0:T(1024)S(1)} %convert_element_type.186, f32[1024]{0:T(1024)S(1)} %fusion.73, f32[1024]{0:T(1024)S(1)} %broadcast_multiply_fusion), kind=kOutput, calls=%fused_computation.196 | convolution fusion | flops 3627024384 | bytes 16133120 | tf_op jit(solution)/shard_map/dot_general | solution.py:201
  382.8 23.6 %all-gather.19.cloned.1.call-done = bf16[1152,768]{1,0:T(8,128)(2,1)} async-done(((bf16[288,768]{1,0:T(8,128)(2,1)}), bf16[1152,768]{1,0:T(8,128)(2,1)}) %all-gather.19.cloned.1.call-update) | async-done | bytes 1769488 | tf_op jit(solution)/shard_map/all_gather | solution.py:149
  406.4 14.5 %fusion.42 = (f32[1024,1152]{1,0:T(8,128)}, f32[1024,1152]{1,0:T(8,128)S(1)}, f32[1024,1152]{1,0:T(8,128)S(1)}) fusion(f32[1024,2304]{1,0:T(8,128)} %fusion.93, bf16[1152,768]{1,0:T(8,128)(2,1)} %all-gather.19.cloned.1.call-done, bf16[1024,768]{0,1:T(8,128)(2,1)S(1)} %copy.75, pred[1024]{0:T(1024)(128)(4,1)S(1)} %get-tuple-element.85, ...), kind=kOutput, calls=%fused_computation.111 | convolution fusion | flops 1890189312 | bytes 22218752 | tf_op jit(solution)/shard_map/td,fd->tf/dot_general | solution.py:221
  420.9 3.5 multiply_add_fusion
  424.4 9.6 multiply_reduce_fusion.2
  437.0 3.3 convolution_convert_fusion.2
  440.3 2.2 fusion.35
  443.6 2.5 convolution_convert_fusion.4
  446.1 2.8 convolution_convert_fusion.3
  449.1 1.8 copy-done.25
  450.8 19.3 %multiply_reduce_fusion.1 = (f32[12,512]{1,0:T(8,128)S(1)}, f32[12,512,1024]{2,1,0:T(8,128)}) fusion(f32[12,512,1024]{2,1,0:T(8,128)} %get-tuple-element.101, f32[12,512]{1,0:T(8,128)S(1)} %get-tuple-element.100, bf16[512,12,64]{0,2,1:T(8,128)(2,1)S(1)} %bitcast.82, bf16[1024,12,64]{0,2,1:T(8,128)(2,1)S(1)} %bitcast.74), kind=kOutput, calls=%fused_computation.9 | convolution fusion | flops 824174592 | bytes 52740096 | tf_op jit(solution)/shard_map/qhd,khd->hqk/dot_general | solution.py:254
  470.1 19.1 %multiply_reduce_fusion = (f32[12,512]{1,0:T(8,128)S(1)}, f32[12,512,1024]{2,1,0:T(8,128)}) fusion(f32[12,512,1024]{2,1,0:T(8,128)} %get-tuple-element.99, f32[12,512]{1,0:T(8,128)S(1)} %get-tuple-element.98, bf16[512,12,64]{0,2,1:T(8,128)(2,1)S(1)} %bitcast.84, bf16[1024,12,64]{0,2,1:T(8,128)(2,1)S(1)} %bitcast.75), kind=kOutput, calls=%fused_computation.7 | convolution fusion | flops 824174592 | bytes 52740096 | tf_op jit(solution)/shard_map/qhd,khd->hqk/dot_general | solution.py:254
  489.3 17.0 %multiply_convert_fusion.1 = bf16[12,512,1024]{2,1,0:T(8,128)(2,1)S(1)} fusion(f32[12,512,1024]{2,1,0:T(8,128)} %get-tuple-element.109, f32[12,512]{1,0:T(8,128)S(1)} %get-tuple-element.108, f32[12,512,1024]{2,1,0:T(8,128)} %get-tuple-element.101, f32[12,512]{1,0:T(8,128)S(1)} %get-tuple-element.100), kind=kLoop, calls=%fused_computation.8 | loop fusion | flops 25165824 | bytes 62963712 | tf_op jit(solution)/shard_map/convert_element_type | solution.py:258
  506.4 27.2 %multiply_convert_fusion = bf16[12,512,1024]{2,1,0:T(8,128)(2,1)} fusion(f32[12,512,1024]{2,1,0:T(8,128)} %get-tuple-element.107, f32[12,512]{1,0:T(8,128)S(1)} %get-tuple-element.106, f32[12,512,1024]{2,1,0:T(8,128)} %get-tuple-element.99, f32[12,512]{1,0:T(8,128)S(1)} %get-tuple-element.98), kind=kLoop, calls=%fused_computation.6 | loop fusion | flops 25165824 | bytes 62963712 | tf_op jit(solution)/shard_map/convert_element_type | solution.py:258
  533.6 2.3 fusion.97
  536.0 9.6 multiply_bitcast_fusion.2
  545.6 9.6 multiply_bitcast_fusion.1
  555.3 7.2 multiply_bitcast_fusion
  562.5 9.7 convolution_convert_fusion
  573.2 3.1 multiply_add_fusion.4
  577.7 10.7 %fusion.10 = f32[12,64,1024]{2,1,0:T(8,128)S(1)} fusion(bf16[512,12,64]{0,2,1:T(8,128)(2,1)S(1)} %bitcast.85, f32[12,512,1024]{2,1,0:T(8,128)} %get-tuple-element.99, f32[12,512]{1,0:T(8,128)S(1)} %get-tuple-element.98), kind=kOutput, calls=%fused_computation.26 | convolution fusion | flops 817889280 | bytes 29122560 | tf_op jit(solution)/shard_map/hqk,qhd->khd/dot_general | solution.py:270
  588.4 10.6 %add_convert_fusion.2 = bf16[12,64,1024]{2,1,0:T(8,128)(2,1)S(1)} fusion(f32[12,64,1024]{2,1,0:T(8,128)S(1)} %fusion.10, bf16[512,12,64]{0,2,1:T(8,128)(2,1)S(1)} %bitcast.83, f32[12,512,1024]{2,1,0:T(8,128)} %get-tuple-element.101, f32[12,512]{1,0:T(8,128)S(1)} %get-tuple-element.100), kind=kOutput, calls=%fused_computation.76 | convolution fusion | flops 819462144 | bytes 30695424 | tf_op jit(solution)/shard_map/hqk,qhd->khd/dot_general | solution.py:270
  600.3 8.7 convolution_convert_fusion.1
  609.1 10.5 %reduce-scatter.9.cloned.1.call-done = bf16[192,2304]{1,0:T(8,128)(2,1)} async-done(((bf16[768,2304]{1,0:T(8,128)(2,1)}), bf16[192,2304]{1,0:T(8,128)(2,1)}) %reduce-scatter.9.cloned.1.call-update) | async-done | bytes 884752 | tf_op jit(solution)/shard_map/reduce_scatter | solution.py:316
  619.6 50.1 %reduce-scatter.5.cloned.1.call-done = bf16[192,2304]{1,0:T(8,128)(2,1)} async-done(((bf16[768,2304]{1,0:T(8,128)(2,1)}), bf16[192,2304]{1,0:T(8,128)(2,1)}) %reduce-scatter.5.cloned.1.call-update) | async-done | bytes 884752 | tf_op jit(solution)/shard_map/reduce_scatter | solution.py:307
  669.8 6.6 add_convert_fusion.5
  676.4 7.2 fusion.34
  686.1 3.0 add_convert_fusion.1
  689.8 8.9 all-reduce.12
  698.9 14.6 %all-reduce.10 = (bf16[192]{0:T(256)(128)(2,1)S(1)}, bf16[192]{0:T(256)(128)(2,1)S(1)}) all-reduce(bf16[192]{0:T(256)(128)(2,1)S(1)} %dynamic-slice.4, bf16[192]{0:T(256)(128)(2,1)S(1)} %dynamic-slice.6), channel_id=1, replica_groups=mesh['replica'=8,'group'=4] {'replica'}, use_global_device_ids=true, to_apply=%region_24.26 | all-reduce | flops 384 | bytes 1536 | tf_op jit(solution)/shard_map/psum | solution.py:324
  714.6 25.9 %all-reduce.16.cloned.1.call-done = (bf16[192,2304]{1,0:T(8,128)(2,1)}, bf16[192,768]{1,0:T(8,128)(2,1)}, bf16[192,2304]{1,0:T(8,128)(2,1)}, bf16[288,768]{1,0:T(8,128)(2,1)}) async-done(((bf16[192,2304]{1,0:T(8,128)(2,1)}, bf16[192,768]{1,0:T(8,128)(2,1)}, bf16[192,2304]{1,0:T(8,128)(2,1)}, bf16[288,768]{1,0:T(8,128)(2,1)}), (bf16[192,2304]{1,0:T(8,128)(2,1)}, bf16[192,768]{1,0:T(8,128)(2,1)}, ...) | async-done | bytes 2506768 | tf_op jit(solution)/shard_map/psum | solution.py:325
  740.5 1.9 convert_element_type.204
  742.4 2.5 convert_element_type.202
  747.2 111.1 %all-gather.23.cloned.1.call-done = bf16[8192,768]{0,1:T(8,128)(2,1)} async-done(((bf16[1024,768]{0,1:T(8,128)(2,1)}), bf16[8192,768]{0,1:T(8,128)(2,1)}) %all-gather.23.cloned.1.call-update) | async-done | bytes 12582928 | tf_op jit(solution)/shard_map/all_gather | solution.py:207
  858.3 16.6 %copy.73 = bf16[8192,768]{1,0:T(8,128)(2,1)} copy(bf16[8192,768]{0,1:T(8,128)(2,1)} %all-gather.23.cloned.1.call-done) | data formatting | bytes 25165824 | tf_op jit(solution)/shard_map/all_gather | solution.py:207
  874.9 10.8 %gather_fusion.1 = bf16[1024,768]{1,0:T(8,128)(2,1)S(1)} fusion(bf16[8192,768]{1,0:T(8,128)(2,1)} %copy.73, s32[1024]{0:T(1024)S(1)} %fusion.75), kind=kCustom, calls=%fused_computation.1.clone | custom fusion | bytes 3149824 | tf_op jit(solution)/shard_map/jit(_take)/gather | solution.py:93
  886.5 88.9 %all-gather.25.cloned.1.call-done = bf16[8192,768]{0,1:T(8,128)(2,1)} async-done(((bf16[1024,768]{0,1:T(8,128)(2,1)}), bf16[8192,768]{0,1:T(8,128)(2,1)}) %all-gather.25.cloned.1.call-update) | async-done | bytes 12582928 | tf_op jit(solution)/shard_map/all_gather | solution.py:293
  975.4 16.7 %copy.76 = bf16[8192,768]{1,0:T(8,128)(2,1)} copy(bf16[8192,768]{0,1:T(8,128)(2,1)} %all-gather.25.cloned.1.call-done) | data formatting | bytes 25165824 | tf_op jit(solution)/shard_map/all_gather | solution.py:293
  992.1 11.8 %gather_fusion.3 = bf16[1024,768]{1,0:T(8,128)(2,1)} fusion(bf16[8192,768]{1,0:T(8,128)(2,1)} %copy.76, s32[1024]{0:T(1024)S(1)} %fusion.75), kind=kCustom, calls=%fused_computation.3.clone | custom fusion | bytes 3149824 | tf_op jit(solution)/shard_map/jit(_take)/gather | solution.py:93
  1003.8 1.7 copy.77
  1005.5 2.0 fusion.40
  1007.6 2.7 copy.79
  (229 shorter events, 34.9 us)
Async XLA Ops:
  7.2 4.3 copy-start.39
  7.2 121.9 %all-gather.11.cloned.1.call-start = ((), (), s32[]{:S(2)}) async-start(), calls=%async_computation.4 | async-start | bytes 14155776 | tf_op jit(solution)/shard_map/all_gather | solution.py:152
  7.9 4.4 copy-start.23
  7.9 169.0 %all-gather.13.cloned.1.call-start = ((), (), s32[]{:S(2)}) async-start(), calls=%async_computation.5 | async-start | bytes 4423680 | tf_op jit(solution)/shard_map/all_gather | solution.py:145
  10.6 284.7 %all-gather.21.cloned.1.call-start = ((), (), s32[]{:S(2)}) async-start(), calls=%async_computation.9 | async-start | bytes 14155776 | tf_op jit(solution)/shard_map/all_gather | solution.py:209
  11.3 3.0 copy-start.59
  11.4 5.1 copy-start.62
  11.4 6.3 copy-start.63
  11.4 8.3 copy-start.65
  11.4 8.3 copy-start.66
  11.4 8.3 copy-start.60
  11.4 311.4 %all-gather.15.cloned.1.call-start = ((), (), s32[]{:S(2)}) async-start(), calls=%async_computation.6 | async-start | bytes 1474560 | tf_op jit(solution)/shard_map/all_gather | solution.py:146
  12.2 360.0 %all-gather.17.cloned.1.call-start = ((), (), s32[]{:S(2)}) async-start(), calls=%async_computation.7 | async-start | bytes 4423680 | tf_op jit(solution)/shard_map/all_gather | solution.py:148
  13.3 393.1 %all-gather.19.cloned.1.call-start = ((), (), s32[]{:S(2)}) async-start(), calls=%async_computation.8 | async-start | bytes 2211840 | tf_op jit(solution)/shard_map/all_gather | solution.py:149
  14.2 594.8 %reduce-scatter.7.cloned.1.call-start = ((), (), s32[]{:S(2)}) async-start(), calls=%async_computation.11 | async-start | bytes 1474560 | tf_op jit(solution)/shard_map/reduce_scatter | solution.py:310
  19.6 420.6 %copy-start.53 = (pred[1024]{0:T(1024)(128)(4,1)}, pred[1024]{0:T(1024)(128)(4,1)S(1)}, u32[]{:S(2)}) copy-start(pred[1024]{0:T(1024)(128)(4,1)S(1)} %get-tuple-element.84) | copy-start | bytes 3076
  19.7 420.6 %copy-start.55 = (pred[1024]{0:T(1024)(128)(4,1)}, pred[1024]{0:T(1024)(128)(4,1)S(1)}, u32[]{:S(2)}) copy-start(pred[1024]{0:T(1024)(128)(4,1)S(1)} %get-tuple-element.85) | copy-start | bytes 3076
  32.8 144.1 %copy-start.43 = (f32[768]{0:T(1024)}, f32[768]{0:T(1024)S(1)}, u32[]{:S(2)}) copy-start(f32[768]{0:T(1024)S(1)} %convert_element_type.173) | copy-start | bytes 9220
  33.4 162.2 %copy-start.29 = (f32[1024,32]{0,1:T(8,128)}, f32[1024,32]{0,1:T(8,128)S(1)}, u32[]{:S(2)}) copy-start(f32[1024,32]{0,1:T(8,128)S(1)} %get-tuple-element.86) | copy-start | bytes 393220
  33.4 162.2 %copy-start.31 = (f32[1024,32]{0,1:T(8,128)}, f32[1024,32]{0,1:T(8,128)S(1)}, u32[]{:S(2)}) copy-start(f32[1024,32]{0,1:T(8,128)S(1)} %get-tuple-element.87) | copy-start | bytes 393220
  140.5 182.2 %copy-start.1 = (bf16[1024,768]{0,1:T(8,128)(2,1)}, bf16[1024,768]{0,1:T(8,128)(2,1)S(1)}, u32[]{:S(2)}) copy-start(bf16[1024,768]{0,1:T(8,128)(2,1)S(1)} %copy.68) | copy-start | bytes 4718596
  141.0 35.9 %copy-start.41 = (f32[1024]{0:T(1024)}, f32[1024]{0:T(1024)S(1)}, u32[]{:S(2)}) copy-start(f32[1024]{0:T(1024)S(1)} %broadcast_multiply_fusion.1) | copy-start | bytes 12292
  141.7 35.2 %copy-start.49 = (f32[1024]{0:T(1024)}, f32[1024]{0:T(1024)S(1)}, u32[]{:S(2)}) copy-start(f32[1024]{0:T(1024)S(1)} %fusion.33) | copy-start | bytes 12292
  141.7 35.2 %copy-start.45 = (f32[1024]{0:T(1024)}, f32[1024]{0:T(1024)S(1)}, u32[]{:S(2)}) copy-start(f32[1024]{0:T(1024)S(1)} %fusion.72) | copy-start | bytes 12292
  199.5 10.5 %copy-start.15 = (bf16[1024,12,32]{0,2,1:T(8,128)(2,1)}, bf16[1024,12,32]{0,2,1:T(8,128)(2,1)S(1)}, u32[]{:S(2)}) copy-start(bf16[1024,12,32]{0,2,1:T(8,128)(2,1)S(1)} %get-tuple-element.74) | copy-start | bytes 2359300
  199.5 10.5 %copy-start.17 = (bf16[1024,12,32]{0,2,1:T(8,128)(2,1)}, bf16[1024,12,32]{0,2,1:T(8,128)(2,1)S(1)}, u32[]{:S(2)}) copy-start(bf16[1024,12,32]{0,2,1:T(8,128)(2,1)S(1)} %get-tuple-element.75) | copy-start | bytes 2359300
  199.6 10.5 %copy-start.8 = (bf16[1024,12,32]{0,2,1:T(8,128)(2,1)}, bf16[1024,12,32]{0,2,1:T(8,128)(2,1)S(1)}, u32[]{:S(2)}) copy-start(bf16[1024,12,32]{0,2,1:T(8,128)(2,1)S(1)} %get-tuple-element.82) | copy-start | bytes 2359300
  199.6 10.5 %copy-start.10 = (bf16[1024,12,32]{0,2,1:T(8,128)(2,1)}, bf16[1024,12,32]{0,2,1:T(8,128)(2,1)S(1)}, u32[]{:S(2)}) copy-start(bf16[1024,12,32]{0,2,1:T(8,128)(2,1)S(1)} %get-tuple-element.83) | copy-start | bytes 2359300
  224.6 33.6 %copy-start.24 = (bf16[1024,768]{0,1:T(8,128)(2,1)S(1)}, bf16[1024,768]{0,1:T(8,128)(2,1)}, u32[]{:S(2)}) copy-start(bf16[1024,768]{0,1:T(8,128)(2,1)} %copy.69) | copy-start | bytes 4718596
  308.8 97.6 %copy-start.5 = (bf16[1024,768]{0,1:T(8,128)(2,1)}, bf16[1024,768]{0,1:T(8,128)(2,1)S(1)}, u32[]{:S(2)}) copy-start(bf16[1024,768]{0,1:T(8,128)(2,1)S(1)} %copy.75) | copy-start | bytes 4718596
  406.4 14.5 %copy-start.19 = (f32[1024,2304]{1,0:T(8,128)S(1)}, f32[1024,2304]{1,0:T(8,128)}, u32[]{:S(2)}) copy-start(f32[1024,2304]{1,0:T(8,128)} %fusion.93) | copy-start | bytes 28311556
  420.8 3.5 copy-start.13
  424.4 9.6 copy-start.21
  434.0 3.0 copy-start.22
  434.8 5.4 copy-start.3
  434.9 5.4 copy-start.47
  440.3 3.4 copy-start.26
  449.0 21.1 %copy-start.35 = (bf16[512,768]{0,1:T(8,128)(2,1)}, bf16[512,768]{0,1:T(8,128)(2,1)S(1)}, u32[]{:S(2)}) copy-start(bf16[512,768]{0,1:T(8,128)(2,1)S(1)} %get-tuple-element.78) | copy-start | bytes 2359300
  449.0 21.1 %copy-start.37 = (bf16[512,768]{0,1:T(8,128)(2,1)}, bf16[512,768]{0,1:T(8,128)(2,1)S(1)}, u32[]{:S(2)}) copy-start(bf16[512,768]{0,1:T(8,128)(2,1)S(1)} %get-tuple-element.79) | copy-start | bytes 2359300
  449.0 160.1 %reduce-scatter.11.cloned.1.call-start = ((), (), s32[]{:S(2)}) async-start(), calls=%async_computation.13 | async-start | bytes 2211840 | tf_op jit(solution)/shard_map/reduce_scatter | solution.py:319
  489.3 130.3 %reduce-scatter.9.cloned.1.call-start = ((), (), s32[]{:S(2)}) async-start(), calls=%async_computation.12 | async-start | bytes 4423680 | tf_op jit(solution)/shard_map/reduce_scatter | solution.py:316
  506.3 27.2 %copy-start = (bf16[12,512,1024]{2,1,0:T(8,128)(2,1)}, bf16[12,512,1024]{2,1,0:T(8,128)(2,1)S(1)}, u32[]{:S(2)}) copy-start(bf16[12,512,1024]{2,1,0:T(8,128)(2,1)S(1)} %multiply_convert_fusion.1) | copy-start | bytes 37748740
  506.4 27.2 %copy-start.9 = (bf16[1024,12,32]{0,2,1:T(8,128)(2,1)S(1)}, bf16[1024,12,32]{0,2,1:T(8,128)(2,1)}, u32[]{:S(2)}) copy-start(bf16[1024,12,32]{0,2,1:T(8,128)(2,1)} %copy-done.8) | copy-start | bytes 2359300
  506.4 27.2 %copy-start.11 = (bf16[1024,12,32]{0,2,1:T(8,128)(2,1)S(1)}, bf16[1024,12,32]{0,2,1:T(8,128)(2,1)}, u32[]{:S(2)}) copy-start(bf16[1024,12,32]{0,2,1:T(8,128)(2,1)} %copy-done.10) | copy-start | bytes 2359300
  555.3 7.2 copy-start.14
  572.3 97.4 %reduce-scatter.5.cloned.1.call-start = ((), (), s32[]{:S(2)}) async-start(), calls=%async_computation.10 | async-start | bytes 4423680 | tf_op jit(solution)/shard_map/reduce_scatter | solution.py:307
  577.7 21.4 %copy-start.27 = (bf16[1024,12,64]{0,2,1:T(8,128)(2,1)}, bf16[1024,12,64]{0,2,1:T(8,128)(2,1)S(1)}, u32[]{:S(2)}) copy-start(bf16[1024,12,64]{0,2,1:T(8,128)(2,1)S(1)} %add_convert_fusion.3) | copy-start | bytes 4718596
  577.7 10.7 %copy-start.36 = (bf16[512,768]{0,1:T(8,128)(2,1)S(1)}, bf16[512,768]{0,1:T(8,128)(2,1)}, u32[]{:S(2)}) copy-start(bf16[512,768]{0,1:T(8,128)(2,1)} %copy-done.35) | copy-start | bytes 2359300
  588.4 11.9 %copy-start.2 = (bf16[1024,768]{0,1:T(8,128)(2,1)S(1)}, bf16[1024,768]{0,1:T(8,128)(2,1)}, u32[]{:S(2)}) copy-start(bf16[1024,768]{0,1:T(8,128)(2,1)} %copy-done.1) | copy-start | bytes 4718596
  588.4 11.9 %copy-start.42 = (f32[1024]{0:T(1024)S(1)}, f32[1024]{0:T(1024)}, u32[]{:S(2)}) copy-start(f32[1024]{0:T(1024)} %copy-done.41) | copy-start | bytes 12292
  588.4 11.9 %copy-start.44 = (f32[768]{0:T(1024)S(1)}, f32[768]{0:T(1024)}, u32[]{:S(2)}) copy-start(f32[768]{0:T(1024)} %copy-done.43) | copy-start | bytes 9220
  588.4 11.8 %copy-start.46 = (f32[1024]{0:T(1024)S(1)}, f32[1024]{0:T(1024)}, u32[]{:S(2)}) copy-start(f32[1024]{0:T(1024)} %copy-done.45) | copy-start | bytes 12292
  588.4 11.8 %copy-start.54 = (pred[1024]{0:T(1024)(128)(4,1)S(1)}, pred[1024]{0:T(1024)(128)(4,1)}, u32[]{:S(2)}) copy-start(pred[1024]{0:T(1024)(128)(4,1)} %copy-done.53) | copy-start | bytes 3076
  588.4 11.8 %copy-start.56 = (pred[1024]{0:T(1024)(128)(4,1)S(1)}, pred[1024]{0:T(1024)(128)(4,1)}, u32[]{:S(2)}) copy-start(pred[1024]{0:T(1024)(128)(4,1)} %copy-done.55) | copy-start | bytes 3076
  609.0 131.5 %all-reduce.16.cloned.1.call-start = ((), (), s32[]{:S(2)}) async-start(), calls=%async_computation.16 | async-start | bytes 5013504 | tf_op jit(solution)/shard_map/psum | solution.py:325
  669.7 188.6 %all-gather.23.cloned.1.call-start = ((), (), s32[]{:S(2)}) async-start(), calls=%async_computation.14 | async-start | bytes 14155776 | tf_op jit(solution)/shard_map/all_gather | solution.py:207
  676.4 7.4 copy-start.50
  676.4 299.0 %all-gather.25.cloned.1.call-start = ((), (), s32[]{:S(2)}) async-start(), calls=%async_computation.15 | async-start | bytes 14155776 | tf_op jit(solution)/shard_map/all_gather | solution.py:293
  686.1 3.7 copy-start.52
  686.1 3.7 copy-start.57
  686.1 3.7 copy-start.58
  686.1 3.7 copy-start.61
  740.5 4.4 copy-start.40
  740.5 5.4 copy-start.34
  (17 other events, 30.3 us)
Sparse Core Ops, SparseCore 0:
  9.6 119.4 all-gather.10
  131.5 45.3 all-gather.12
  178.5 116.6 all-gather.20
  297.0 25.7 all-gather.14
  325.0 47.1 all-gather.16
  373.9 32.4 all-gather.18
  449.2 28.7 reduce-scatter.6
  489.4 32.4 reduce-scatter.10
  572.4 47.1 reduce-scatter.8
  622.5 47.1 reduce-scatter.4
  672.4 68.0 all-reduce.15
  742.0 116.3 all-gather.22
  860.5 114.8 all-gather.24
where the time goes:
time: 1030 us; the launch traced here: 1020 us
  waiting for transfers between devices  510 us (50%)
  matrix products  222 us (22%)
  other arithmetic  122 us (12%)
  local copies, waits for them, and re-layouts  113 us (11%)
  blocking collectives  34.9 us (3%)
  between operations  16.4 us (2%)
    all_gather x1, waiting for transfers between devices, on_device(): lax.all_gather(output_dealt[None], 'replica', axis=1, tiled=True)  111 us
    all_gather x1, waiting for transfers between devices, on_device(): lax.all_gather(tokens, 'replica', axis=1, tiled=True)  94.1 us
    all_gather x1, waiting for transfers between devices, on_device(): lax.all_gather(grad_input[None], 'replica', axis=1, tiled=True)  88.9 us
    reduce_scatter x1, waiting for transfers between devices, on_device(): lax.psum_scatter(partial_grads[1].astype(jnp.bfloat16), 'group', scatter_...  50.1 us
    gather x8, local copies, waits for them, and re-layouts, pick_rows(): taken = jnp.take(piece[0], jnp.clip(index_map, 0, piece_rows - 1), axis=0)  49.9 us
    convert_element_type x2, other arithmetic, on_device(): grad_scores = (weights_full * (grad_probs - inner)).astype(jnp.bfloat16)  44.2 us
    all_gather x1, waiting for transfers between devices, on_device(): lax.all_gather(masters[4], 'group', axis=0, tiled=True)  44 us
    dot_general x2, matrix products, on_device(): jnp.einsum('qhd,khd->hqk', grad_block, value_heads, preferred_element_typ...  38.4 us
  transfers between devices with their start and end apart: 13, of which 11 were waited for; matrix products, arithmetic and copies ran while one was open for 36% of the time, Pallas kernels for 0%

commit v1 on v0

--- a/solution.py
+++ b/solution.py
@@ -9,6 +9,27 @@
 epsilon = 1e-05
 big_negative = -1e30
 rope_base = 160000.0
+
+
+def ring_gather(value, axis, dim):
+    size, index, rows = (lax.axis_size(axis), lax.axis_index(axis), value.shape[dim])
+    right = [(i, (i + 1) % size) for i in range(size)]
+    left = [(i, (i - 1) % size) for i in range(size)]
+    out = jnp.zeros((*value.shape[:dim], size * rows, *value.shape[dim + 1 :]), value.dtype)
+    out = lax.dynamic_update_slice_in_dim(out, value, index * rows, axis=dim)
+    from_left = from_right = value
+    half = size // 2
+    for step in range(1, half + 1):
+        from_left = lax.ppermute(from_left, axis, right)
+        out = lax.dynamic_update_slice_in_dim(
+            out, from_left, (index - step) % size * rows, axis=dim
+        )
+        if step < size - half:
+            from_right = lax.ppermute(from_right, axis, left)
+            out = lax.dynamic_update_slice_in_dim(
+                out, from_right, (index + step) % size * rows, axis=dim
+            )
+    return out
 
 
 def column_starts(lengths):
@@ -142,7 +163,7 @@
     )
     weights = (
         lax.all_gather(masters[0], "group", axis=0, tiled=True),
-        lax.all_gather(masters[1], "group", axis=0, tiled=True),
+        ring_gather(masters[1], "group", 0),
         lax.all_gather(masters[2], "group", axis=0, tiled=True),
         lax.all_gather(masters[3], "group", axis=0, tiled=True),
         lax.all_gather(masters[4], "group", axis=0, tiled=True),

time: 1030 us -> 1030 us (level)
  waiting for transfers between devices: 510 us -> 475 us
  other arithmetic: 122 us -> 134 us
  local copies, waits for them, and re-layouts: 113 us -> 125 us
    all_gather x1, waiting for transfers between devices: 94.1 us -> 42.3 us  [on_device(): lax.all_gather(tokens, 'replica', axis=1, tiled=True)]
    ppermute x0 -> x3, waiting for transfers between devices: none -> 18.2 us  [the longest x2 18.2 us: ring_gather(): from_left = lax.ppermute(from_left, axis, right)]
    all_gather x1, waiting for transfers between devices: 14.1 us -> 0.02 us  [on_device(): lax.all_gather(cotangent, 'replica', axis=1, tiled=True)]
    unnamed x146 -> x140, local copies, waits for them, and re-layouts: 16.7 us -> 22.4 us
  transfers between devices with their start and end apart: 13 -> 16, of which waited for: 11 -> 11; matrix products, arithmetic and copies ran while one was open for 36% -> 38% of each run, Pallas kernels for 0% -> 0%
where the time goes in v1:
time: 1030 us; the launch traced here: 1020 us
  waiting for transfers between devices  475 us (46%)
  matrix products  221 us (21%)
  other arithmetic  134 us (13%)
  local copies, waits for them, and re-layouts  125 us (12%)
  blocking collectives  43.7 us (4%)
  between operations  16.6 us (2%)
    all_gather x1, waiting for transfers between devices, on_device(): lax.all_gather(output_dealt[None], 'replica', axis=1, tiled=True)  111 us
    all_gather x1, waiting for transfers between devices, on_device(): lax.all_gather(grad_input[None], 'replica', axis=1, tiled=True)  88.9 us
    gather x8, local copies, waits for them, and re-layouts, pick_rows(): taken = jnp.take(piece[0], jnp.clip(index_map, 0, piece_rows - 1), axis=0)  50.6 us
    reduce_scatter x1, waiting for transfers between devices, on_device(): lax.psum_scatter(partial_grads[1].astype(jnp.bfloat16), 'group', scatter_...  50.3 us
    all_gather x1, waiting for transfers between devices, on_device(): lax.all_gather(masters[4], 'group', axis=0, tiled=True)  44 us
    convert_element_type x2, other arithmetic, on_device(): grad_scores = (weights_full * (grad_probs - inner)).astype(jnp.bfloat16)  43.9 us
    all_gather x1, waiting for transfers between devices, on_device(): lax.all_gather(masters[1], 'group', axis=0, tiled=True)  42.7 us
    all_gather x1, waiting for transfers between devices, on_device(): lax.all_gather(tokens, 'replica', axis=1, tiled=True)  42.3 us
  transfers between devices with their start and end apart: 16, of which 11 were waited for; matrix products, arithmetic and copies ran while one was open for 38% of the time, Pallas kernels for 0%

profile of v1, /device:TPU:0, one launch (start us, length us, event | category | flops | bytes accessed | tf_op | source)
XLA Modules:
  0.0 1019.2 jit_solution(2682324507903221928)
XLA Ops:
  10.9 2.5 constant_dynamic-update-slice_fusion.3
  13.4 3.9 collective-permute-start.1
  17.3 2.0 convert_element_type.190
  41.1 20.1 %all-reduce.13 = (bf16[768]{0:T(1024)(128)(2,1)}, bf16[768]{0:T(1024)(128)(2,1)}) all-reduce(bf16[768]{0:T(1024)(128)(2,1)} %dynamic-update-slice, bf16[768]{0:T(1024)(128)(2,1)} %dynamic-update-slice.1), channel_id=1, replica_groups=mesh['replica'=8,'group'=4] {'group'}, use_global_device_ids=true, to_apply=%add.6 | all-reduce | flops 1536 | bytes 6144
  63.1 2.3 broadcast_compare_fusion.1
  68.5 18.2 %collective-permute-done.2 = bf16[192,2304]{1,0:T(8,128)(2,1)S(1)} collective-permute-done((bf16[192,2304]{1,0:T(8,128)(2,1)}, bf16[192,2304]{1,0:T(8,128)(2,1)S(1)}, u32[]{:S(2)}, u32[]{:S(2)}) %collective-permute-start.2) | collective-permute-done | bytes 884768 | tf_op jit(solution)/shard_map/ppermute | solution.py:23
  86.8 42.3 %all-gather.11.cloned.1.call-done = bf16[1,8192,768]{2,1,0:T(8,128)(2,1)} async-done(((bf16[1,1024,768]{2,1,0:T(8,128)(2,1)}), bf16[1,8192,768]{2,1,0:T(8,128)(2,1)}) %all-gather.11.cloned.1.call-update) | async-done | bytes 12582928 | tf_op jit(solution)/shard_map/all_gather | solution.py:173
  129.1 11.4 %gather_fusion = bf16[1024,768]{1,0:T(8,128)(2,1)S(1)} fusion(bf16[8192,768]{1,0:T(8,128)(2,1)} %bitcast.69, s32[1024]{0:T(1024)} %get-tuple-element.95), kind=kCustom, calls=%fused_computation.clone | custom fusion | bytes 3149824 | tf_op jit(solution)/shard_map/jit(_take)/gather | solution.py:114
  143.6 6.2 fusion.60
  150.0 3.1 fusion.104
  153.1 3.6 copy.71
  158.3 3.7 copy.70
  161.9 4.0 subtract_convert_fusion
  166.0 10.3 %fusion.62 = f32[12,512,1024]{2,1,0:T(8,128)} fusion(bf16[1024,12,32]{0,2,1:T(8,128)(2,1)S(1)} %get-tuple-element.84, bf16[1024,12,32]{0,2,1:T(8,128)(2,1)S(1)} %get-tuple-element.85, bf16[1024,12,32]{0,2,1:T(8,128)(2,1)S(1)} %get-tuple-element.77, bf16[1024,12,32]{0,2,1:T(8,128)(2,1)S(1)} %get-tuple-element.76), kind=kOutput, calls=%fused_computation.126 | convolution fusion | flops 810024960 | bytes 28311552 | tf_op jit(solution)/shard_map/qhd,khd->hqk/dot_general | solution.py:120
  176.3 15.1 %fusion.109 = (f32[12,512]{1,0:T(8,128)S(1)}, f32[12,512,1024]{2,1,0:T(8,128)}) fusion(pred[512,1024]{1,0:T(8,128)(4,1)} %get-tuple-element.90, bf16[1024,12,32]{0,2,1:T(8,128)(2,1)} %copy-done.17, bf16[1024,12,32]{0,2,1:T(8,128)(2,1)} %copy-done.15, bf16[1024,12,32]{0,2,1:T(8,128)(2,1)S(1)} %get-tuple-element.85, ...), kind=kOutput, calls=%fused_computation.209 | convolution fusion | flops 835191808 | bytes 28860416 | tf_op jit(solution)/shard_map/sub | solution.py:210
  191.3 33.6 %fusion.108 = (f32[12,512]{1,0:T(8,128)S(1)}, f32[12,512,1024]{2,1,0:T(8,128)}) fusion(f32[12,512,1024]{2,1,0:T(8,128)} %fusion.62, pred[512,1024]{1,0:T(8,128)(4,1)} %get-tuple-element.91), kind=kOutput, calls=%fused_computation.208 | output fusion | flops 37749760 | bytes 50880512 | tf_op jit(solution)/shard_map/sub | solution.py:210
  224.9 11.3 %fusion.52 = bf16[512,12,64]{0,2,1:T(8,128)(2,1)} fusion(bf16[1024,12,64]{0,2,1:T(8,128)(2,1)S(1)} %bitcast.72, f32[12,512,1024]{2,1,0:T(8,128)} %get-tuple-element.103, f32[12,512]{1,0:T(8,128)S(1)} %get-tuple-element.102), kind=kOutput, calls=%fused_computation.115 | convolution fusion | flops 818282496 | bytes 27549696 | tf_op jit(solution)/shard_map/hqk,khd->qhd/dot_general | solution.py:213
  236.2 11.4 %fusion.49 = bf16[512,12,64]{0,2,1:T(8,128)(2,1)} fusion(bf16[1024,12,64]{0,2,1:T(8,128)(2,1)S(1)} %bitcast.73, f32[12,512,1024]{2,1,0:T(8,128)} %get-tuple-element.101, f32[12,512]{1,0:T(8,128)S(1)} %get-tuple-element.100), kind=kOutput, calls=%fused_computation.114 | convolution fusion | flops 818282496 | bytes 27549696 | tf_op jit(solution)/shard_map/hqk,khd->qhd/dot_general | solution.py:213
  247.7 11.8 %gather_fusion.2 = bf16[1024,768]{1,0:T(8,128)(2,1)} fusion(bf16[8192,768]{1,0:T(8,128)(2,1)} %bitcast.68, s32[1024]{0:T(1024)S(1)} %copy-done.57), kind=kCustom, calls=%fused_computation.2.clone | custom fusion | bytes 3149824 | tf_op jit(solution)/shard_map/jit(_take)/gather | solution.py:114
  261.2 3.3 pad_maximum_fusion.5
  264.4 8.9 all-gather.13.cloned.1.call-done
  273.3 3.4 fusion.114
  278.8 44.0 %all-gather.15.cloned.1.call-done = bf16[768,2304]{1,0:T(8,128)(2,1)} async-done(((bf16[192,2304]{1,0:T(8,128)(2,1)}), bf16[768,2304]{1,0:T(8,128)(2,1)}) %all-gather.15.cloned.1.call-update) | async-done | bytes 3538960 | tf_op jit(solution)/shard_map/all_gather | solution.py:169
  322.8 10.6 %fusion.93 = f32[1024,2304]{1,0:T(8,128)} fusion(bf16[768,2304]{1,0:T(8,128)(2,1)} %all-gather.15.cloned.1.call-done, f32[1024,768]{0,1:T(8,128)} %copy-done.12, f32[768]{0:T(1024)S(1)} %copy-done.58, f32[1024]{0:T(1024)S(1)} %fusion.73, f32[1024]{0:T(1024)S(1)} %broadcast_multiply_fusion), kind=kOutput, calls=%fused_computation.200 | convolution fusion | flops 3627024384 | bytes 16133120 | tf_op jit(solution)/shard_map/dot_general | solution.py:222
  333.3 23.6 %all-gather.17.cloned.1.call-done = bf16[1152,768]{1,0:T(8,128)(2,1)} async-done(((bf16[288,768]{1,0:T(8,128)(2,1)}), bf16[1152,768]{1,0:T(8,128)(2,1)}) %all-gather.17.cloned.1.call-update) | async-done | bytes 1769488 | tf_op jit(solution)/shard_map/all_gather | solution.py:170
  356.9 14.3 %fusion.42 = (f32[1024,1152]{1,0:T(8,128)}, f32[1024,1152]{1,0:T(8,128)S(1)}, f32[1024,1152]{1,0:T(8,128)S(1)}) fusion(f32[1024,2304]{1,0:T(8,128)} %fusion.93, bf16[1152,768]{1,0:T(8,128)(2,1)} %all-gather.17.cloned.1.call-done, bf16[1024,768]{0,1:T(8,128)(2,1)S(1)} %copy.75, pred[1024]{0:T(1024)(128)(4,1)S(1)} %copy-done.55, ...), kind=kOutput, calls=%fused_computation.111 | convolution fusion | flops 1890189312 | bytes 22218752 | tf_op jit(solution)/shard_map/td,fd->tf/dot_general | solution.py:242
  371.2 3.9 multiply_add_fusion
  375.2 9.6 multiply_reduce_fusion.2
  387.8 3.3 convolution_convert_fusion.2
  391.1 2.2 fusion.35
  394.4 2.5 convolution_convert_fusion.4
  397.0 2.8 convolution_convert_fusion.3
  401.7 19.3 %multiply_reduce_fusion.1 = (f32[12,512]{1,0:T(8,128)S(1)}, f32[12,512,1024]{2,1,0:T(8,128)}) fusion(f32[12,512,1024]{2,1,0:T(8,128)} %get-tuple-element.103, f32[12,512]{1,0:T(8,128)S(1)} %get-tuple-element.102, bf16[512,12,64]{0,2,1:T(8,128)(2,1)S(1)} %bitcast.82, bf16[1024,12,64]{0,2,1:T(8,128)(2,1)S(1)} %bitcast.74), kind=kOutput, calls=%fused_computation.9 | convolution fusion | flops 824174592 | bytes 52740096 | tf_op jit(solution)/shard_map/qhd,khd->hqk/dot_general | solution.py:275
  421.0 19.1 %multiply_reduce_fusion = (f32[12,512]{1,0:T(8,128)S(1)}, f32[12,512,1024]{2,1,0:T(8,128)}) fusion(f32[12,512,1024]{2,1,0:T(8,128)} %get-tuple-element.101, f32[12,512]{1,0:T(8,128)S(1)} %get-tuple-element.100, bf16[512,12,64]{0,2,1:T(8,128)(2,1)S(1)} %bitcast.84, bf16[1024,12,64]{0,2,1:T(8,128)(2,1)S(1)} %bitcast.75), kind=kOutput, calls=%fused_computation.7 | convolution fusion | flops 824174592 | bytes 52740096 | tf_op jit(solution)/shard_map/qhd,khd->hqk/dot_general | solution.py:275
  440.2 17.0 %multiply_convert_fusion.1 = bf16[12,512,1024]{2,1,0:T(8,128)(2,1)S(1)} fusion(f32[12,512,1024]{2,1,0:T(8,128)} %get-tuple-element.111, f32[12,512]{1,0:T(8,128)S(1)} %get-tuple-element.110, f32[12,512,1024]{2,1,0:T(8,128)} %get-tuple-element.103, f32[12,512]{1,0:T(8,128)S(1)} %get-tuple-element.102), kind=kLoop, calls=%fused_computation.8 | loop fusion | flops 25165824 | bytes 62963712 | tf_op jit(solution)/shard_map/convert_element_type | solution.py:279
  457.3 26.9 %multiply_convert_fusion = bf16[12,512,1024]{2,1,0:T(8,128)(2,1)} fusion(f32[12,512,1024]{2,1,0:T(8,128)} %get-tuple-element.109, f32[12,512]{1,0:T(8,128)S(1)} %get-tuple-element.108, f32[12,512,1024]{2,1,0:T(8,128)} %get-tuple-element.101, f32[12,512]{1,0:T(8,128)S(1)} %get-tuple-element.100), kind=kLoop, calls=%fused_computation.6 | loop fusion | flops 25165824 | bytes 62963712 | tf_op jit(solution)/shard_map/convert_element_type | solution.py:279
  484.2 2.3 fusion.97
  486.6 9.6 multiply_bitcast_fusion.2
  496.2 9.6 multiply_bitcast_fusion.1
  505.9 7.2 multiply_bitcast_fusion
  513.1 9.8 convolution_convert_fusion
  523.9 3.0 multiply_add_fusion.4
  528.3 10.7 %fusion.10 = f32[12,64,1024]{2,1,0:T(8,128)S(1)} fusion(bf16[512,12,64]{0,2,1:T(8,128)(2,1)S(1)} %bitcast.85, f32[12,512,1024]{2,1,0:T(8,128)} %get-tuple-element.101, f32[12,512]{1,0:T(8,128)S(1)} %get-tuple-element.100), kind=kOutput, calls=%fused_computation.26 | convolution fusion | flops 817889280 | bytes 29122560 | tf_op jit(solution)/shard_map/hqk,qhd->khd/dot_general | solution.py:291
  539.1 10.6 %add_convert_fusion.2 = bf16[12,64,1024]{2,1,0:T(8,128)(2,1)S(1)} fusion(f32[12,64,1024]{2,1,0:T(8,128)S(1)} %fusion.10, bf16[512,12,64]{0,2,1:T(8,128)(2,1)S(1)} %bitcast.83, f32[12,512,1024]{2,1,0:T(8,128)} %get-tuple-element.103, f32[12,512]{1,0:T(8,128)S(1)} %get-tuple-element.102), kind=kOutput, calls=%fused_computation.76 | convolution fusion | flops 819462144 | bytes 30695424 | tf_op jit(solution)/shard_map/hqk,qhd->khd/dot_general | solution.py:291
  550.9 8.7 convolution_convert_fusion.1
  560.3 9.9 reduce-scatter.9.cloned.1.call-done
  570.2 50.3 %reduce-scatter.5.cloned.1.call-done = bf16[192,2304]{1,0:T(8,128)(2,1)} async-done(((bf16[768,2304]{1,0:T(8,128)(2,1)}), bf16[192,2304]{1,0:T(8,128)(2,1)}) %reduce-scatter.5.cloned.1.call-update) | async-done | bytes 884752 | tf_op jit(solution)/shard_map/reduce_scatter | solution.py:328
  620.6 6.6 add_convert_fusion.5
  627.3 42.7 %all-gather.21.cloned.1.call-done = bf16[768,2304]{1,0:T(8,128)(2,1)} async-done(((bf16[192,2304]{1,0:T(8,128)(2,1)}), bf16[768,2304]{1,0:T(8,128)(2,1)}) %all-gather.21.cloned.1.call-update) | async-done | bytes 3538960 | tf_op jit(solution)/shard_map/all_gather | solution.py:233
  670.0 7.0 fusion.34
  679.6 3.0 add_convert_fusion.1
  683.5 8.9 all-reduce.12
  692.6 14.7 %all-reduce.10 = (bf16[192]{0:T(256)(128)(2,1)S(1)}, bf16[192]{0:T(256)(128)(2,1)S(1)}) all-reduce(bf16[192]{0:T(256)(128)(2,1)S(1)} %dynamic-slice.4, bf16[192]{0:T(256)(128)(2,1)S(1)} %dynamic-slice.6), channel_id=1, replica_groups=mesh['replica'=8,'group'=4] {'replica'}, use_global_device_ids=true, to_apply=%region_24.26 | all-reduce | flops 384 | bytes 1536 | tf_op jit(solution)/shard_map/psum | solution.py:345
  708.4 32.5 %all-reduce.16.cloned.1.call-done = (bf16[192,2304]{1,0:T(8,128)(2,1)}, bf16[192,768]{1,0:T(8,128)(2,1)}, bf16[192,2304]{1,0:T(8,128)(2,1)}, bf16[288,768]{1,0:T(8,128)(2,1)}) async-done(((bf16[192,2304]{1,0:T(8,128)(2,1)}, bf16[192,768]{1,0:T(8,128)(2,1)}, bf16[192,2304]{1,0:T(8,128)(2,1)}, bf16[288,768]{1,0:T(8,128)(2,1)}), (bf16[192,2304]{1,0:T(8,128)(2,1)}, bf16[192,768]{1,0:T(8,128)(2,1)}, ...) | async-done | bytes 2506768 | tf_op jit(solution)/shard_map/psum | solution.py:346
  740.9 1.9 convert_element_type.204
  742.8 2.5 convert_element_type.202
  747.6 111.1 %all-gather.23.cloned.1.call-done = bf16[8192,768]{0,1:T(8,128)(2,1)} async-done(((bf16[1024,768]{0,1:T(8,128)(2,1)}), bf16[8192,768]{0,1:T(8,128)(2,1)}) %all-gather.23.cloned.1.call-update) | async-done | bytes 12582928 | tf_op jit(solution)/shard_map/all_gather | solution.py:228
  858.7 16.6 %copy.73 = bf16[8192,768]{1,0:T(8,128)(2,1)} copy(bf16[8192,768]{0,1:T(8,128)(2,1)} %all-gather.23.cloned.1.call-done) | data formatting | bytes 25165824 | tf_op jit(solution)/shard_map/all_gather | solution.py:228
  875.4 10.8 %gather_fusion.1 = bf16[1024,768]{1,0:T(8,128)(2,1)S(1)} fusion(bf16[8192,768]{1,0:T(8,128)(2,1)} %copy.73, s32[1024]{0:T(1024)S(1)} %fusion.75), kind=kCustom, calls=%fused_computation.1.clone | custom fusion | bytes 3149824 | tf_op jit(solution)/shard_map/jit(_take)/gather | solution.py:114
  886.9 88.9 %all-gather.25.cloned.1.call-done = bf16[8192,768]{0,1:T(8,128)(2,1)} async-done(((bf16[1024,768]{0,1:T(8,128)(2,1)}), bf16[8192,768]{0,1:T(8,128)(2,1)}) %all-gather.25.cloned.1.call-update) | async-done | bytes 12582928 | tf_op jit(solution)/shard_map/all_gather | solution.py:314
  975.8 16.7 %copy.76 = bf16[8192,768]{1,0:T(8,128)(2,1)} copy(bf16[8192,768]{0,1:T(8,128)(2,1)} %all-gather.25.cloned.1.call-done) | data formatting | bytes 25165824 | tf_op jit(solution)/shard_map/all_gather | solution.py:314
  992.5 11.8 %gather_fusion.3 = bf16[1024,768]{1,0:T(8,128)(2,1)} fusion(bf16[8192,768]{1,0:T(8,128)(2,1)} %copy.76, s32[1024]{0:T(1024)S(1)} %fusion.75), kind=kCustom, calls=%fused_computation.3.clone | custom fusion | bytes 3149824 | tf_op jit(solution)/shard_map/jit(_take)/gather | solution.py:114
  1005.9 2.0 fusion.40
  1008.0 2.7 copy.79
  (233 shorter events, 59.1 us)
Async XLA Ops:
  7.2 121.9 %all-gather.11.cloned.1.call-start = ((), (), s32[]{:S(2)}) async-start(), calls=%async_computation.4 | async-start | bytes 14155776 | tf_op jit(solution)/shard_map/all_gather | solution.py:173
  7.9 239.7 %all-gather.19.cloned.1.call-start = ((), (), s32[]{:S(2)}) async-start(), calls=%async_computation.8 | async-start | bytes 14155776 | tf_op jit(solution)/shard_map/all_gather | solution.py:230
  8.7 264.7 %all-gather.13.cloned.1.call-start = ((), (), s32[]{:S(2)}) async-start(), calls=%async_computation.5 | async-start | bytes 1474560 | tf_op jit(solution)/shard_map/all_gather | solution.py:167
  9.5 313.3 %all-gather.15.cloned.1.call-start = ((), (), s32[]{:S(2)}) async-start(), calls=%async_computation.6 | async-start | bytes 4423680 | tf_op jit(solution)/shard_map/all_gather | solution.py:169
  10.6 346.4 %all-gather.17.cloned.1.call-start = ((), (), s32[]{:S(2)}) async-start(), calls=%async_computation.7 | async-start | bytes 2211840 | tf_op jit(solution)/shard_map/all_gather | solution.py:170
  10.9 8.5 copy-start.62
  13.4 53.8 %collective-permute-start.1 = (bf16[192,2304]{1,0:T(8,128)(2,1)}, bf16[192,2304]{1,0:T(8,128)(2,1)}, u32[]{:S(2)}, u32[]{:S(2)}) collective-permute-start(bf16[192,2304]{1,0:T(8,128)(2,1)} %get-tuple-element.67), channel_id=1, source_target_pairs={{0,3},{1,0},{2,1},{3,2},{4,7},{5,4},{6,5},{7,6},{8,11},{9,8},{10,9... | collective-permute-start | bytes 2654216 | tf_op jit(solution)/shard_map/ppermute | solution.py:28
  17.3 48.1 %collective-permute-start = (bf16[192,2304]{1,0:T(8,128)(2,1)}, bf16[192,2304]{1,0:T(8,128)(2,1)}, u32[]{:S(2)}, u32[]{:S(2)}) collective-permute-start(bf16[192,2304]{1,0:T(8,128)(2,1)} %get-tuple-element.67), channel_id=1, source_target_pairs={{0,1},{1,2},{2,3},{3,0},{4,5},{5,6},{6,7},{7,4},{8,9},{9,10},{10,1... | collective-permute-start | bytes 2654216 | tf_op jit(solution)/shard_map/ppermute | solution.py:23
  19.3 541.0 %reduce-scatter.7.cloned.1.call-start = ((), (), s32[]{:S(2)}) async-start(), calls=%async_computation.11 | async-start | bytes 1474560 | tf_op jit(solution)/shard_map/reduce_scatter | solution.py:331
  28.3 32.8 %copy-start.51 = (s32[1024]{0:T(1024)}, s32[1024]{0:T(1024)S(1)}, u32[]{:S(2)}) copy-start(s32[1024]{0:T(1024)S(1)} %get-tuple-element.46) | copy-start | bytes 12292
  61.8 80.6 %copy-start.43 = (f32[768]{0:T(1024)}, f32[768]{0:T(1024)S(1)}, u32[]{:S(2)}) copy-start(f32[768]{0:T(1024)S(1)} %convert_element_type.173) | copy-start | bytes 9220
  65.4 21.3 %collective-permute-start.2 = (bf16[192,2304]{1,0:T(8,128)(2,1)}, bf16[192,2304]{1,0:T(8,128)(2,1)S(1)}, u32[]{:S(2)}, u32[]{:S(2)}) collective-permute-start(bf16[192,2304]{1,0:T(8,128)(2,1)} %collective-permute-done), channel_id=1, source_target_pairs={{0,1},{1,2},{2,3},{3,0},{4,5},{5,6},{6,7},{7,4},{8,9},{9,10},{10,1... | collective-permute-start | bytes 2654216 | tf_op jit(solution)/shard_map/ppermute | solution.py:23
  66.0 325.1 %copy-start.53 = (pred[1024]{0:T(1024)(128)(4,1)}, pred[1024]{0:T(1024)(128)(4,1)S(1)}, u32[]{:S(2)}) copy-start(pred[1024]{0:T(1024)(128)(4,1)S(1)} %get-tuple-element.86) | copy-start | bytes 3076
  86.8 42.3 %copy-start.22 = (bf16[768,2304]{1,0:T(8,128)(2,1)}, bf16[768,2304]{1,0:T(8,128)(2,1)S(1)}, u32[]{:S(2)}) copy-start(bf16[768,2304]{1,0:T(8,128)(2,1)S(1)} %constant_dynamic-update-slice_fusion) | copy-start | bytes 10616836
  141.3 132.1 %copy-start.1 = (bf16[1024,768]{0,1:T(8,128)(2,1)}, bf16[1024,768]{0,1:T(8,128)(2,1)S(1)}, u32[]{:S(2)}) copy-start(bf16[1024,768]{0,1:T(8,128)(2,1)S(1)} %copy.68) | copy-start | bytes 4718596
  141.8 8.0 copy-start.41
  158.3 3.7 copy-start.30
  158.3 3.7 copy-start.32
  165.9 10.3 %copy-start.15 = (bf16[1024,12,32]{0,2,1:T(8,128)(2,1)}, bf16[1024,12,32]{0,2,1:T(8,128)(2,1)S(1)}, u32[]{:S(2)}) copy-start(bf16[1024,12,32]{0,2,1:T(8,128)(2,1)S(1)} %get-tuple-element.76) | copy-start | bytes 2359300
  165.9 10.3 %copy-start.17 = (bf16[1024,12,32]{0,2,1:T(8,128)(2,1)}, bf16[1024,12,32]{0,2,1:T(8,128)(2,1)S(1)}, u32[]{:S(2)}) copy-start(bf16[1024,12,32]{0,2,1:T(8,128)(2,1)S(1)} %get-tuple-element.77) | copy-start | bytes 2359300
  165.9 10.3 %copy-start.8 = (bf16[1024,12,32]{0,2,1:T(8,128)(2,1)}, bf16[1024,12,32]{0,2,1:T(8,128)(2,1)S(1)}, u32[]{:S(2)}) copy-start(bf16[1024,12,32]{0,2,1:T(8,128)(2,1)S(1)} %get-tuple-element.84) | copy-start | bytes 2359300
  166.0 10.3 %copy-start.10 = (bf16[1024,12,32]{0,2,1:T(8,128)(2,1)}, bf16[1024,12,32]{0,2,1:T(8,128)(2,1)S(1)}, u32[]{:S(2)}) copy-start(bf16[1024,12,32]{0,2,1:T(8,128)(2,1)S(1)} %get-tuple-element.85) | copy-start | bytes 2359300
  191.3 33.6 %copy-start.25 = (bf16[1024,768]{0,1:T(8,128)(2,1)S(1)}, bf16[1024,768]{0,1:T(8,128)(2,1)}, u32[]{:S(2)}) copy-start(bf16[1024,768]{0,1:T(8,128)(2,1)} %copy.69) | copy-start | bytes 4718596
  236.2 11.5 %copy-start.57 = (s32[1024]{0:T(1024)S(1)}, s32[1024]{0:T(1024)}, u32[]{:S(2)}) copy-start(s32[1024]{0:T(1024)} %get-tuple-element.95) | copy-start | bytes 12292
  261.2 95.8 %copy-start.5 = (bf16[1024,768]{0,1:T(8,128)(2,1)}, bf16[1024,768]{0,1:T(8,128)(2,1)S(1)}, u32[]{:S(2)}) copy-start(bf16[1024,768]{0,1:T(8,128)(2,1)S(1)} %copy.75) | copy-start | bytes 4718596
  276.8 46.0 %copy-start.58 = (f32[768]{0:T(1024)S(1)}, f32[768]{0:T(1024)}, u32[]{:S(2)}) copy-start(f32[768]{0:T(1024)} %convert_element_type.186) | copy-start | bytes 9220
  356.9 14.3 %copy-start.19 = (f32[1024,2304]{1,0:T(8,128)S(1)}, f32[1024,2304]{1,0:T(8,128)}, u32[]{:S(2)}) copy-start(f32[1024,2304]{1,0:T(8,128)} %fusion.93) | copy-start | bytes 28311556
  371.2 3.9 copy-start.13
  375.2 9.6 copy-start.21
  384.8 3.0 copy-start.23
  385.6 5.5 copy-start.3
  385.6 5.5 copy-start.47
  391.1 3.3 copy-start.27
  399.9 21.1 %copy-start.35 = (bf16[512,768]{0,1:T(8,128)(2,1)}, bf16[512,768]{0,1:T(8,128)(2,1)S(1)}, u32[]{:S(2)}) copy-start(bf16[512,768]{0,1:T(8,128)(2,1)S(1)} %get-tuple-element.80) | copy-start | bytes 2359300
  399.9 21.1 %copy-start.37 = (bf16[512,768]{0,1:T(8,128)(2,1)}, bf16[512,768]{0,1:T(8,128)(2,1)S(1)}, u32[]{:S(2)}) copy-start(bf16[512,768]{0,1:T(8,128)(2,1)S(1)} %get-tuple-element.81) | copy-start | bytes 2359300
  399.9 160.4 %reduce-scatter.11.cloned.1.call-start = ((), (), s32[]{:S(2)}) async-start(), calls=%async_computation.13 | async-start | bytes 2211840 | tf_op jit(solution)/shard_map/reduce_scatter | solution.py:340
  440.1 130.1 %reduce-scatter.9.cloned.1.call-start = ((), (), s32[]{:S(2)}) async-start(), calls=%async_computation.12 | async-start | bytes 4423680 | tf_op jit(solution)/shard_map/reduce_scatter | solution.py:337
  457.2 27.0 %copy-start = (bf16[12,512,1024]{2,1,0:T(8,128)(2,1)}, bf16[12,512,1024]{2,1,0:T(8,128)(2,1)S(1)}, u32[]{:S(2)}) copy-start(bf16[12,512,1024]{2,1,0:T(8,128)(2,1)S(1)} %multiply_convert_fusion.1) | copy-start | bytes 37748740
  457.2 27.0 %copy-start.9 = (bf16[1024,12,32]{0,2,1:T(8,128)(2,1)S(1)}, bf16[1024,12,32]{0,2,1:T(8,128)(2,1)}, u32[]{:S(2)}) copy-start(bf16[1024,12,32]{0,2,1:T(8,128)(2,1)} %copy-done.8) | copy-start | bytes 2359300
  457.2 27.0 %copy-start.11 = (bf16[1024,12,32]{0,2,1:T(8,128)(2,1)S(1)}, bf16[1024,12,32]{0,2,1:T(8,128)(2,1)}, u32[]{:S(2)}) copy-start(bf16[1024,12,32]{0,2,1:T(8,128)(2,1)} %copy-done.10) | copy-start | bytes 2359300
  505.9 7.2 copy-start.14
  522.9 97.6 %reduce-scatter.5.cloned.1.call-start = ((), (), s32[]{:S(2)}) async-start(), calls=%async_computation.10 | async-start | bytes 4423680 | tf_op jit(solution)/shard_map/reduce_scatter | solution.py:328
  528.3 21.4 %copy-start.28 = (bf16[1024,12,64]{0,2,1:T(8,128)(2,1)}, bf16[1024,12,64]{0,2,1:T(8,128)(2,1)S(1)}, u32[]{:S(2)}) copy-start(bf16[1024,12,64]{0,2,1:T(8,128)(2,1)S(1)} %add_convert_fusion.3) | copy-start | bytes 4718596
  528.3 10.7 %copy-start.36 = (bf16[512,768]{0,1:T(8,128)(2,1)S(1)}, bf16[512,768]{0,1:T(8,128)(2,1)}, u32[]{:S(2)}) copy-start(bf16[512,768]{0,1:T(8,128)(2,1)} %copy-done.35) | copy-start | bytes 2359300
  539.0 11.9 %copy-start.2 = (bf16[1024,768]{0,1:T(8,128)(2,1)S(1)}, bf16[1024,768]{0,1:T(8,128)(2,1)}, u32[]{:S(2)}) copy-start(bf16[1024,768]{0,1:T(8,128)(2,1)} %copy-done.1) | copy-start | bytes 4718596
  539.0 11.8 %copy-start.42 = (f32[1024]{0:T(1024)S(1)}, f32[1024]{0:T(1024)}, u32[]{:S(2)}) copy-start(f32[1024]{0:T(1024)} %copy-done.41) | copy-start | bytes 12292
  539.0 11.8 %copy-start.44 = (f32[768]{0:T(1024)S(1)}, f32[768]{0:T(1024)}, u32[]{:S(2)}) copy-start(f32[768]{0:T(1024)} %copy-done.43) | copy-start | bytes 9220
  539.0 11.8 %copy-start.46 = (f32[1024]{0:T(1024)S(1)}, f32[1024]{0:T(1024)}, u32[]{:S(2)}) copy-start(f32[1024]{0:T(1024)} %copy-done.45) | copy-start | bytes 12292
  539.0 11.8 %copy-start.54 = (pred[1024]{0:T(1024)(128)(4,1)S(1)}, pred[1024]{0:T(1024)(128)(4,1)}, u32[]{:S(2)}) copy-start(pred[1024]{0:T(1024)(128)(4,1)} %copy-done.53) | copy-start | bytes 3076
  539.0 11.8 %copy-start.56 = (pred[1024]{0:T(1024)(128)(4,1)S(1)}, pred[1024]{0:T(1024)(128)(4,1)}, u32[]{:S(2)}) copy-start(pred[1024]{0:T(1024)(128)(4,1)} %get-tuple-element.87) | copy-start | bytes 3076
  559.6 110.3 %all-gather.21.cloned.1.call-start = ((), (), s32[]{:S(2)}) async-start(), calls=%async_computation.9 | async-start | bytes 4423680 | tf_op jit(solution)/shard_map/all_gather | solution.py:233
  560.2 180.7 %all-reduce.16.cloned.1.call-start = ((), (), s32[]{:S(2)}) async-start(), calls=%async_computation.16 | async-start | bytes 5013504 | tf_op jit(solution)/shard_map/psum | solution.py:346
  620.6 238.1 %all-gather.23.cloned.1.call-start = ((), (), s32[]{:S(2)}) async-start(), calls=%async_computation.14 | async-start | bytes 14155776 | tf_op jit(solution)/shard_map/all_gather | solution.py:228
  627.2 49.8 %copy-start.50 = (f32[1024]{0:T(1024)S(1)}, f32[1024]{0:T(1024)}, u32[]{:S(2)}) copy-start(f32[1024]{0:T(1024)} %copy-done.49) | copy-start | bytes 12292
  627.2 348.6 %all-gather.25.cloned.1.call-start = ((), (), s32[]{:S(2)}) async-start(), calls=%async_computation.15 | async-start | bytes 14155776 | tf_op jit(solution)/shard_map/all_gather | solution.py:314
  677.0 2.6 copy-start.7
  677.0 2.6 copy-start.48
  679.6 3.8 copy-start.52
  679.6 3.8 copy-start.59
  679.6 3.8 copy-start.60
  679.6 3.8 copy-start.61
  740.9 4.4 copy-start.40
  740.9 5.4 copy-start.34
  1008.0 2.7 copy-start.20
  (17 other events, 25.6 us)
Sparse Core Ops, SparseCore 0:
  9.6 119.4 all-gather.10
  130.7 114.8 all-gather.18
  247.5 25.7 all-gather.12
  275.6 47.1 all-gather.14
  324.4 32.4 all-gather.16
  400.0 28.6 reduce-scatter.6
  440.3 32.4 reduce-scatter.10
  523.1 47.1 reduce-scatter.8
  573.3 47.1 reduce-scatter.4
  622.8 47.1 all-gather.20
  672.6 68.2 all-reduce.15
  742.4 116.3 all-gather.22
  860.9 114.8 all-gather.24
